TPU v7x, 32 devices: a whole 2x2x4 slice. The times are simulated.
32 devices in a mesh: ctx: 8 (over y, x, core), tp: 4 (over z).
Axes of the slice: x: 2, y: 2, z: 4, core: 2. Of those that a mesh axis runs over, the one named last changes fastest.
Arguments:
- queries: bfloat16 [4096, 64, 128], P('ctx', 'tp'), may hold values from -5 to 5
- own_keys: bfloat16 [4096, 8, 128], P('ctx', 'tp'), may hold values from -5 to 5
- own_values: bfloat16 [4096, 8, 128], P('ctx', 'tp'), may hold values from -5 to 5
- cache_keys: bfloat16 [8, 32768, 128], P('tp', 'ctx'), may hold values from -5 to 5
- cache_values: bfloat16 [8, 32768, 128], P('tp', 'ctx'), may hold values from -5 to 5
- selected: int32 [8, 8, 8], P('ctx', 'tp'), may hold values from 0 to 63, as said below
- out_weight: bfloat16 [8192, 8192], P('tp'), may hold values from -0.0625 to 0.0625
Outputs:
- mixed: bfloat16 [4096, 8192], P('ctx', 'tp')
Inputs may be any that keep to these rules, and one draw needn't show every extreme that they name: `selected`: for each query block and key head, 8 different cache blocks, each lying in the cache of a different index of ctx (blocks k * 8 to (k + 1) * 8 - 1 for index k), so that at most 1 of them lie in one index.
All inputs are finite; a program needn't handle non-finite values.
Results may differ from a plain program's by a relative error of at most 0.017.
Values may be sent and summed in bfloat16 or wider, within the bound.
A program may use at most 192 MiB of HBM per device.

v0:
```python
import jax
import jax.numpy as jnp
from jax import lax
from jax.sharding import PartitionSpec as P

CAPB = 1


def attend(query_block, key_set, value_set):
    rows_count, heads_count, head_width = query_block.shape
    total_keys = key_set.shape[0]
    remote_count = total_keys - rows_count
    column = lax.broadcasted_iota(jnp.int32, (rows_count, total_keys), 1)
    row_index = lax.broadcasted_iota(jnp.int32, (rows_count, total_keys), 0)
    allowed = (column < remote_count) | (column - remote_count <= row_index)
    paired_all = jnp.transpose(query_block, (1, 0, 2)).reshape(
        heads_count // 2, 2, rows_count, head_width
    )

    def one_pair(paired):
        scores = jnp.einsum("gtd,kd->gtk", paired, key_set, preferred_element_type=jnp.float32)
        scores = scores * head_width ** (-0.5)
        scores = jnp.where(allowed[None], scores, -jnp.inf)
        largest = jnp.max(scores, axis=2, keepdims=True)
        powers = jnp.exp(scores - largest)
        weights = (powers / jnp.sum(powers, axis=2, keepdims=True)).astype(jnp.bfloat16)
        return jnp.einsum(
            "gtk,kd->gtd", weights, value_set, preferred_element_type=jnp.float32
        ).astype(jnp.bfloat16)

    result = lax.map(one_pair, paired_all).reshape(heads_count, rows_count, head_width)
    return jnp.transpose(result, (1, 0, 2))


def shards(queries, own_keys, own_values, cache_keys, cache_values, selected, out_weight):
    block_rows = queries.shape[0]
    kv_local = cache_keys.shape[0]
    head_width = cache_keys.shape[2]
    blocks_dev = cache_keys.shape[1] // block_rows
    picked = selected[0]
    picked_count = picked.shape[1]
    owner_count = lax.axis_size("ctx")
    head_range = jnp.arange(kv_local, dtype=jnp.int32)[:, None]
    owner_of = picked // blocks_dev
    inside = picked % blocks_dev
    earlier = jnp.arange(picked_count)[None, :] < jnp.arange(picked_count)[:, None]
    same_owner = owner_of[:, :, None] == owner_of[:, None, :]
    ranking = jnp.sum(same_owner & earlier[None], axis=2)
    local_ids = head_range * blocks_dev + inside
    owner_match = (
        owner_of[:, :, None, None] == jnp.arange(owner_count, dtype=jnp.int32)[None, None, :, None]
    )
    slot_match = ranking[:, :, None, None] == jnp.arange(CAPB, dtype=jnp.int32)[None, None, None, :]
    request = jnp.sum(jnp.where(owner_match & slot_match, local_ids[:, :, None, None], 0), axis=1)
    request = jnp.transpose(request, (1, 0, 2))
    flat_keys = cache_keys.reshape(kv_local * blocks_dev, block_rows, head_width)
    flat_values = cache_values.reshape(kv_local * blocks_dev, block_rows, head_width)
    wanted = lax.all_to_all(request, "ctx", split_axis=0, concat_axis=0, tiled=True)
    got_keys = lax.all_to_all(flat_keys[wanted], "ctx", split_axis=0, concat_axis=0, tiled=True)
    got_values = lax.all_to_all(flat_values[wanted], "ctx", split_axis=0, concat_axis=0, tiled=True)
    position = owner_of * CAPB + ranking
    key_blocks = []
    value_blocks = []
    for kv_head in range(kv_local):
        key_blocks.append(
            got_keys[:, kv_head].reshape(owner_count * CAPB, block_rows, head_width)[
                position[kv_head]
            ]
        )
        value_blocks.append(
            got_values[:, kv_head].reshape(owner_count * CAPB, block_rows, head_width)[
                position[kv_head]
            ]
        )
    group_size = queries.shape[1] // kv_local
    outputs = []
    for kv_head in range(kv_local):
        key_set = jnp.concatenate(
            [
                key_blocks[kv_head].reshape(picked_count * block_rows, head_width),
                own_keys[:, kv_head],
            ],
            axis=0,
        )
        value_set = jnp.concatenate(
            [
                value_blocks[kv_head].reshape(picked_count * block_rows, head_width),
                own_values[:, kv_head],
            ],
            axis=0,
        )
        outputs.append(
            attend(
                queries[:, kv_head * group_size : (kv_head + 1) * group_size], key_set, value_set
            )
        )
    attended = jnp.concatenate(outputs, axis=1).reshape(block_rows, queries.shape[1] * head_width)
    partial_term = jnp.dot(attended, out_weight, preferred_element_type=jnp.float32).astype(
        jnp.bfloat16
    )
    return (
        lax.psum_scatter(partial_term, "tp", scatter_dimension=1, tiled=True)
        .astype(jnp.float32)
        .astype(jnp.bfloat16)
    )


def solution(mesh):
    in_specs = (
        P("ctx", "tp", None),
        P("ctx", "tp", None),
        P("ctx", "tp", None),
        P("tp", "ctx", None),
        P("tp", "ctx", None),
        P("ctx", "tp", None),
        P("tp", None),
    )
    out_specs = P("ctx", "tp")
    return jax.shard_map(shards, mesh=mesh, in_specs=in_specs, out_specs=out_specs, check_vma=False)
```

profile of v0, /device:TPU:0, one launch (start us, length us, event | category | flops | bytes accessed | tf_op | source)
XLA Modules:
  0.0 538.1 jit_solution(2003307089156999809)
XLA Ops:
  7.8 9.7 %all_to_all.15 = s32[8,2,1]{1,2,0:T(1,128)S(1)} all-to-all(s32[8,2,1]{1,2,0:T(1,128)S(1)} %copy.34), channel_id=1, replica_groups=mesh['ctx'=8,'tp'=4] {'ctx'}, dimensions={0} | all-to-all | bytes 128 | tf_op jit(solution)/shard_map/all_to_all | solution.py:58
  17.6 2.1 gather_fusion
  19.8 3.6 all-to-all-start.1
  23.4 3.7 gather_fusion.2
  27.1 22.8 %all-to-all-done.1 = bf16[8,2,1,512,128]{4,3,1,2,0:T(8,128)(2,1)S(1)} async-done(((bf16[8,2,1,512,128]{4,3,1,2,0:T(8,128)(2,1)}), bf16[8,2,1,512,128]{4,3,1,2,0:T(8,128)(2,1)S(1)}, u32[]{:S(2)}, u32[]{:S(2)}) %all-to-all-start.1) | async-done | bytes 2097184 | tf_op jit(solution)/shard_map/all_to_all | solution.py:59
  49.9 4.3 all-to-all-start.2
  54.3 2.6 slice_bitcast_fusion.5
  57.0 2.4 copy.33
  64.8 2.0 gather_fusion.1
  66.8 14.1 %all-to-all-done.2 = bf16[8,2,1,512,128]{4,3,1,2,0:T(8,128)(2,1)} async-done(((bf16[8,2,1,512,128]{4,3,1,2,0:T(8,128)(2,1)}), bf16[8,2,1,512,128]{4,3,1,2,0:T(8,128)(2,1)}, u32[]{:S(2)}, u32[]{:S(2)}) %all-to-all-start.2) | async-done | bytes 2097184 | tf_op jit(solution)/shard_map/all_to_all | solution.py:60
  80.9 2.8 slice_bitcast_fusion.2
  88.8 131.2 %while.22 = (s32[]{:T(128)}, bf16[4,2,512,128]{2,3,1,0:T(8,128)(2,1)}, bf16[4,2,512,128]{3,2,1,0:T(8,128)(2,1)}, bf16[4608,128]{1,0:T(8,128)(2,1)S(1)}, bf16[460...) while((s32[]{:T(128)}, ...), condition=%wide.region_5.6_spmd.clone, body=%wide.region_2.5_spmd.clone.sunk | while | flops 2458522112 | bytes 84180568 | solution.py:31
  89.0 3.6 fusion.70
  92.6 3.0 fusion.71
  95.6 16.0 %fusion.72 = (f32[2,512]{1,0:T(2,128)S(1)}, f32[2,512,4608]{2,1,0:T(8,128)}) fusion(f32[2,512,4608]{2,1,0:T(8,128)S(1)} %fusion.70, pred[512,4608]{1,0:T(8,128)(4,1)} %fusion.71), kind=kOutput, calls=%fused_computation.95.clone.1 | output fusion | flops 28316160 | bytes 40112128 | tf_op jit(solution)/shard_map/while/body/eval_jaxpr/sub | solution.py:25
  111.6 9.3 %fusion.73 = bf16[1,2,512,128]{3,2,1,0:T(8,128)(2,1)S(1)} fusion(bf16[4608,128]{1,0:T(8,128)(2,1)} %get-tuple-element.297, f32[2,512,4608]{2,1,0:T(8,128)} %get-tuple-element.242, f32[2,512]{1,0:T(2,128)S(1)} %get-tuple-element.243), kind=kOutput, calls=%fused_computation.23.clone.1 | convolution fusion | flops 1217527808 | bytes 20320256 | tf_op jit(solution)/shard_map/while/body/eval_jaxpr/gtk,kd->gtd/dot_general | solution.py:27
  121.8 3.6 fusion.70
  125.3 3.0 fusion.71
  128.4 16.0 %fusion.72 = (f32[2,512]{1,0:T(2,128)S(1)}, f32[2,512,4608]{2,1,0:T(8,128)}) fusion(f32[2,512,4608]{2,1,0:T(8,128)S(1)} %fusion.70, pred[512,4608]{1,0:T(8,128)(4,1)} %fusion.71), kind=kOutput, calls=%fused_computation.95.clone.1 | output fusion | flops 28316160 | bytes 40112128 | tf_op jit(solution)/shard_map/while/body/eval_jaxpr/sub | solution.py:25
  144.4 9.3 %fusion.73 = bf16[1,2,512,128]{3,2,1,0:T(8,128)(2,1)S(1)} fusion(bf16[4608,128]{1,0:T(8,128)(2,1)} %get-tuple-element.297, f32[2,512,4608]{2,1,0:T(8,128)} %get-tuple-element.242, f32[2,512]{1,0:T(2,128)S(1)} %get-tuple-element.243), kind=kOutput, calls=%fused_computation.23.clone.1 | convolution fusion | flops 1217527808 | bytes 20320256 | tf_op jit(solution)/shard_map/while/body/eval_jaxpr/gtk,kd->gtd/dot_general | solution.py:27
  154.5 3.6 fusion.70
  158.1 3.0 fusion.71
  161.1 16.0 %fusion.72 = (f32[2,512]{1,0:T(2,128)S(1)}, f32[2,512,4608]{2,1,0:T(8,128)}) fusion(f32[2,512,4608]{2,1,0:T(8,128)S(1)} %fusion.70, pred[512,4608]{1,0:T(8,128)(4,1)} %fusion.71), kind=kOutput, calls=%fused_computation.95.clone.1 | output fusion | flops 28316160 | bytes 40112128 | tf_op jit(solution)/shard_map/while/body/eval_jaxpr/sub | solution.py:25
  177.1 9.3 %fusion.73 = bf16[1,2,512,128]{3,2,1,0:T(8,128)(2,1)S(1)} fusion(bf16[4608,128]{1,0:T(8,128)(2,1)} %get-tuple-element.297, f32[2,512,4608]{2,1,0:T(8,128)} %get-tuple-element.242, f32[2,512]{1,0:T(2,128)S(1)} %get-tuple-element.243), kind=kOutput, calls=%fused_computation.23.clone.1 | convolution fusion | flops 1217527808 | bytes 20320256 | tf_op jit(solution)/shard_map/while/body/eval_jaxpr/gtk,kd->gtd/dot_general | solution.py:27
  187.3 3.6 fusion.70
  190.9 3.0 fusion.71
  193.9 16.0 %fusion.72 = (f32[2,512]{1,0:T(2,128)S(1)}, f32[2,512,4608]{2,1,0:T(8,128)}) fusion(f32[2,512,4608]{2,1,0:T(8,128)S(1)} %fusion.70, pred[512,4608]{1,0:T(8,128)(4,1)} %fusion.71), kind=kOutput, calls=%fused_computation.95.clone.1 | output fusion | flops 28316160 | bytes 40112128 | tf_op jit(solution)/shard_map/while/body/eval_jaxpr/sub | solution.py:25
  209.9 9.3 %fusion.73 = bf16[1,2,512,128]{3,2,1,0:T(8,128)(2,1)S(1)} fusion(bf16[4608,128]{1,0:T(8,128)(2,1)} %get-tuple-element.297, f32[2,512,4608]{2,1,0:T(8,128)} %get-tuple-element.242, f32[2,512]{1,0:T(2,128)S(1)} %get-tuple-element.243), kind=kOutput, calls=%fused_computation.23.clone.1 | convolution fusion | flops 1217527808 | bytes 20320256 | tf_op jit(solution)/shard_map/while/body/eval_jaxpr/gtk,kd->gtd/dot_general | solution.py:27
  220.1 3.1 gather_fusion.4
  227.7 131.2 %while.23 = (s32[]{:T(128)}, bf16[4,2,512,128]{2,3,1,0:T(8,128)(2,1)}, bf16[4,2,512,128]{3,2,1,0:T(8,128)(2,1)}, bf16[4608,128]{1,0:T(8,128)(2,1)S(1)}, bf16[460...) while((s32[]{:T(128)}, ...), condition=%wide.region_9.10_spmd.clone, body=%wide.region_6.9_spmd.clone.sunk | while | flops 2458522112 | bytes 84180568 | solution.py:31
  227.9 3.6 fusion.77
  231.5 3.0 fusion.78
  234.5 16.0 %fusion.79 = (f32[2,512]{1,0:T(2,128)S(1)}, f32[2,512,4608]{2,1,0:T(8,128)}) fusion(f32[2,512,4608]{2,1,0:T(8,128)S(1)} %fusion.77, pred[512,4608]{1,0:T(8,128)(4,1)} %fusion.78), kind=kOutput, calls=%fused_computation.96.clone.1 | output fusion | flops 28316160 | bytes 40112128 | tf_op jit(solution)/shard_map/while/body/eval_jaxpr/sub | solution.py:25
  250.5 9.3 %fusion.80 = bf16[1,2,512,128]{3,2,1,0:T(8,128)(2,1)S(1)} fusion(bf16[4608,128]{1,0:T(8,128)(2,1)} %get-tuple-element.273, f32[2,512,4608]{2,1,0:T(8,128)} %get-tuple-element.251, f32[2,512]{1,0:T(2,128)S(1)} %get-tuple-element.252), kind=kOutput, calls=%fused_computation.45.clone.1 | convolution fusion | flops 1217527808 | bytes 20320256 | tf_op jit(solution)/shard_map/while/body/eval_jaxpr/gtk,kd->gtd/dot_general | solution.py:27
  260.6 3.6 fusion.77
  264.2 3.0 fusion.78
  267.2 16.0 %fusion.79 = (f32[2,512]{1,0:T(2,128)S(1)}, f32[2,512,4608]{2,1,0:T(8,128)}) fusion(f32[2,512,4608]{2,1,0:T(8,128)S(1)} %fusion.77, pred[512,4608]{1,0:T(8,128)(4,1)} %fusion.78), kind=kOutput, calls=%fused_computation.96.clone.1 | output fusion | flops 28316160 | bytes 40112128 | tf_op jit(solution)/shard_map/while/body/eval_jaxpr/sub | solution.py:25
  283.2 9.3 %fusion.80 = bf16[1,2,512,128]{3,2,1,0:T(8,128)(2,1)S(1)} fusion(bf16[4608,128]{1,0:T(8,128)(2,1)} %get-tuple-element.273, f32[2,512,4608]{2,1,0:T(8,128)} %get-tuple-element.251, f32[2,512]{1,0:T(2,128)S(1)} %get-tuple-element.252), kind=kOutput, calls=%fused_computation.45.clone.1 | convolution fusion | flops 1217527808 | bytes 20320256 | tf_op jit(solution)/shard_map/while/body/eval_jaxpr/gtk,kd->gtd/dot_general | solution.py:27
  293.4 3.6 fusion.77
  297.0 3.0 fusion.78
  300.0 16.0 %fusion.79 = (f32[2,512]{1,0:T(2,128)S(1)}, f32[2,512,4608]{2,1,0:T(8,128)}) fusion(f32[2,512,4608]{2,1,0:T(8,128)S(1)} %fusion.77, pred[512,4608]{1,0:T(8,128)(4,1)} %fusion.78), kind=kOutput, calls=%fused_computation.96.clone.1 | output fusion | flops 28316160 | bytes 40112128 | tf_op jit(solution)/shard_map/while/body/eval_jaxpr/sub | solution.py:25
  316.0 9.3 %fusion.80 = bf16[1,2,512,128]{3,2,1,0:T(8,128)(2,1)S(1)} fusion(bf16[4608,128]{1,0:T(8,128)(2,1)} %get-tuple-element.273, f32[2,512,4608]{2,1,0:T(8,128)} %get-tuple-element.251, f32[2,512]{1,0:T(2,128)S(1)} %get-tuple-element.252), kind=kOutput, calls=%fused_computation.45.clone.1 | convolution fusion | flops 1217527808 | bytes 20320256 | tf_op jit(solution)/shard_map/while/body/eval_jaxpr/gtk,kd->gtd/dot_general | solution.py:27
  326.2 3.6 fusion.77
  329.7 3.0 fusion.78
  332.8 16.0 %fusion.79 = (f32[2,512]{1,0:T(2,128)S(1)}, f32[2,512,4608]{2,1,0:T(8,128)}) fusion(f32[2,512,4608]{2,1,0:T(8,128)S(1)} %fusion.77, pred[512,4608]{1,0:T(8,128)(4,1)} %fusion.78), kind=kOutput, calls=%fused_computation.96.clone.1 | output fusion | flops 28316160 | bytes 40112128 | tf_op jit(solution)/shard_map/while/body/eval_jaxpr/sub | solution.py:25
  348.7 9.3 %fusion.80 = bf16[1,2,512,128]{3,2,1,0:T(8,128)(2,1)S(1)} fusion(bf16[4608,128]{1,0:T(8,128)(2,1)} %get-tuple-element.273, f32[2,512,4608]{2,1,0:T(8,128)} %get-tuple-element.251, f32[2,512]{1,0:T(2,128)S(1)} %get-tuple-element.252), kind=kOutput, calls=%fused_computation.45.clone.1 | convolution fusion | flops 1217527808 | bytes 20320256 | tf_op jit(solution)/shard_map/while/body/eval_jaxpr/gtk,kd->gtd/dot_general | solution.py:27
  360.6 26.0 %convolution_convert_fusion = bf16[512,8192]{1,0:T(8,128)(2,1)} fusion(bf16[512,2048]{0,1:T(8,128)(2,1)S(1)} %bitcast.123, bf16[2048,8192]{1,0:T(8,128)(2,1)} %param.17), kind=kOutput, calls=%fused_computation.52 | convolution fusion | flops 17184063488 | bytes 44040192 | tf_op jit(solution)/shard_map/dot_general | solution.py:98
  386.7 144.2 %reduce-scatter.2.cloned.1.call-done = bf16[512,2048]{1,0:T(8,128)(2,1)} async-done(((bf16[512,8192]{1,0:T(8,128)(2,1)}), bf16[512,2048]{1,0:T(8,128)(2,1)}) %reduce-scatter.2.cloned.1.call-update) | async-done | bytes 2097168 | tf_op jit(solution)/shard_map/reduce_scatter | solution.py:102
  (64 shorter events, 25.1 us)
Async XLA Ops:
  6.5 11.1 %copy-start = (bf16[2,4096,128]{2,1,0:T(8,128)(2,1)S(1)}, bf16[2,4096,128]{2,1,0:T(8,128)(2,1)}, u32[]{:S(2)}) copy-start(bf16[2,4096,128]{2,1,0:T(8,128)(2,1)} %param.14) | copy-start | bytes 6291460
  19.8 30.2 %all-to-all-start.1 = ((bf16[8,2,1,512,128]{4,3,1,2,0:T(8,128)(2,1)}), bf16[8,2,1,512,128]{4,3,1,2,0:T(8,128)(2,1)S(1)}, u32[]{:S(2)}, u32[]{:S(2)}) async-start(bf16[8,2,1,512,128]{4,3,1,2,0:T(8,128)(2,1)} %bitcast.113), calls=%async_computation.1 | async-start | bytes 4194304 | tf_op jit(solution)/shard_map/all_to_all | solution.py:59
  49.9 31.0 %all-to-all-start.2 = ((bf16[8,2,1,512,128]{4,3,1,2,0:T(8,128)(2,1)}), bf16[8,2,1,512,128]{4,3,1,2,0:T(8,128)(2,1)}, u32[]{:S(2)}, u32[]{:S(2)}) async-start(bf16[8,2,1,512,128]{4,3,1,2,0:T(8,128)(2,1)} %bitcast.13), calls=%async_computation.2 | async-start | bytes 4194304 | tf_op jit(solution)/shard_map/all_to_all | solution.py:60
  54.3 476.5 %reduce-scatter.2.cloned.1.call-start = ((), (), s32[]{:S(2)}) async-start(), calls=%async_computation.4 | async-start | bytes 10485760 | tf_op jit(solution)/shard_map/reduce_scatter | solution.py:102
  57.0 4.2 copy-start.4
  59.4 2.8 copy-start.5
  85.4 1.2 copy-start.2
  220.1 3.1 copy-start.3
  220.1 4.1 copy-start.6
  223.2 2.3 copy-start.7
  386.6 144.2 %copy-start.1 = (bf16[2,4096,128]{2,1,0:T(8,128)(2,1)S(1)}, bf16[2,4096,128]{2,1,0:T(8,128)(2,1)}, u32[]{:S(2)}) copy-start(bf16[2,4096,128]{2,1,0:T(8,128)(2,1)} %param.14) | copy-start | bytes 6291460
Sparse Core Ops, SparseCore 0:
  386.8 143.9 reduce-scatter.1
where the time goes:
time: 542 us; the launch traced here: 538 us
  waiting for transfers between devices  181 us (33%)
  other arithmetic  159 us (29%)
  matrix products  129 us (24%)
  local copies, waits for them, and re-layouts  36.7 us (7%)
  between operations  13.9 us (3%)
  blocking collectives  9.68 us (2%)
  starting transfers between devices  7.99 us (1%)
    reduce_scatter x1, waiting for transfers between devices, shards(): lax.psum_scatter(partial_term, 'tp', scatter_dimension=1, tiled=True)  144 us
    sub x8, other arithmetic, one_pair(): powers = jnp.exp(scores - largest)  128 us
    dot_general x8, matrix products, one_pair(): jnp.einsum('gtk,kd->gtd', weights, value_set, preferred_element_type=jnp....  74.3 us
    dot_general x8, matrix products, one_pair(): jnp.einsum('gtd,kd->gtk', paired, key_set, preferred_element_type=jnp.flo...  28.5 us
    dot_general x1, matrix products, shards(): jnp.dot(attended, out_weight, preferred_element_type=jnp.float32)  26 us
    or x8, other arithmetic, attend(): allowed = (column < remote_count) | (column - remote_count <= row_index)  24.2 us
    all_to_all x1, waiting for transfers between devices, shards(): lax.all_to_all(flat_keys[wanted], 'ctx', split_axis=0, concat_axis=0, til...  22.8 us
    all_to_all x1, waiting for transfers between devices, shards(): lax.all_to_all(flat_values[wanted], 'ctx', split_axis=0, concat_axis=0, t...  14.1 us
  transfers between devices with their start and end apart: 3, of which 3 were waited for; matrix products, arithmetic and copies ran while one was open for 3% of the time, Pallas kernels for 0%

commit v1 on v0

v1 whole, which is shorter than its diff:
```python
import functools

import jax
import jax.numpy as jnp
from jax import lax
from jax.experimental import pallas as pl
from jax.experimental.pallas import tpu as pltpu
from jax.sharding import PartitionSpec as P

LOG2E = 1.4426950408889634


def attention_kernel(start, group, owner_ref, query_ref, own_keys, own_values, got, out_ref,
                     keys, values, scores_a, scores_b, peaks, powers_a, powers_b, total, sems):
    rows, width = query_ref.shape
    head_width = own_keys.shape[-1]
    kv_local = own_keys.shape[0]
    picked = owner_ref.shape[1]
    block = got.shape[3]
    stop = start + rows
    cached = picked * block
    units = width // head_width
    factor = head_width ** -0.5 * LOG2E

    copies = []
    for head in range(kv_local):
        for slot in range(picked):
            place = pl.ds(slot * block, block)
            owner = owner_ref[head, slot]
            copies.append(pltpu.make_async_copy(got.at[owner, head, 0], keys.at[head, place], sems.at[len(copies)]))
            copies.append(pltpu.make_async_copy(
                got.at[owner, head, 1], values.at[head, place, pl.ds(0, head_width)], sems.at[len(copies)]))
        place = pl.ds(cached, stop)
        copies.append(pltpu.make_async_copy(own_keys.at[head, pl.ds(0, stop)], keys.at[head, place], sems.at[len(copies)]))
        copies.append(pltpu.make_async_copy(
            own_values.at[head, pl.ds(0, stop)], values.at[head, place, pl.ds(0, head_width)], sems.at[len(copies)]))
    for copy in copies:
        copy.start()
    for head in range(kv_local):
        values[head, :, head_width:] = jnp.ones((cached + stop, head_width), jnp.bfloat16)
    for copy in copies:
        copy.wait()

    step = 2 * block
    cuts = [(first, min(step, cached - first)) for first in range(0, cached, step)] + [(cached, stop)]

    def phase(unit, scores_now, scores_next, powers_now, powers_before, stages=(True, True, True)):
        ahead, middle, last = stages
        following = unit + 1
        before = unit - 1
        if ahead:
            query = query_ref[:, pl.ds(pl.multiple_of(following * head_width, head_width), head_width)]
            next_head = following // group
        if middle:
            peak = peaks[...]
        if last:
            before_head = before // group
        lanes = None
        for index, (first, size) in enumerate(cuts):
            if ahead:
                part = lax.dot_general(query, keys[next_head, first:first + size], (((1,), (1,)), ((), ())),
                                       preferred_element_type=jnp.float32)
                if first == cached:
                    row = lax.broadcasted_iota(jnp.int32, part.shape, 0)
                    column = lax.broadcasted_iota(jnp.int32, part.shape, 1)
                    part = jnp.where(column <= row + start, part, -jnp.inf)
                scores_next[:, first:first + size] = part
                for lane in range(0, size, head_width):
                    piece = part[:, lane:lane + head_width]
                    lanes = piece if lanes is None else jnp.maximum(lanes, piece)
            if middle:
                for lane in range(first, first + size, head_width):
                    powers_now[:, lane:lane + head_width] = jnp.exp2(
                        (scores_now[:, lane:lane + head_width] - peak) * factor).astype(jnp.bfloat16)
            if last:
                term = jnp.dot(powers_before[:, first:first + size], values[before_head, first:first + size],
                               preferred_element_type=jnp.float32)
                if index == 0:
                    total[...] = term
                elif index < len(cuts) - 1:
                    total[...] += term
                else:
                    term = total[...] + term
                    out_ref[:, pl.ds(pl.multiple_of(before * head_width, head_width), head_width)] = (
                        term[:, :head_width] / term[:, head_width:]).astype(jnp.bfloat16)
        if ahead:
            peaks[...] = jnp.broadcast_to(jnp.max(lanes, axis=1, keepdims=True), peaks.shape)

    phase(-1, scores_a, scores_b, powers_a, powers_b, (True, False, False))
    phase(0, scores_b, scores_a, powers_b, powers_a, (True, True, False))

    def pair(index, carry):
        phase(2 * index + 1, scores_a, scores_b, powers_a, powers_b)
        phase(2 * index + 2, scores_b, scores_a, powers_b, powers_a)
        return carry

    lax.fori_loop(0, units // 2 - 1, pair, 0)
    phase(units - 1, scores_a, scores_b, powers_a, powers_b, (False, True, True))
    phase(units, scores_b, scores_a, powers_b, powers_a, (False, False, True))


def attend(start, group, owners, query, own_keys, own_values, got):
    rows = query.shape[0]
    head_width = own_keys.shape[-1]
    kv_local = own_keys.shape[0]
    picked = owners.shape[1]
    block = got.shape[3]
    count = picked * block + start + rows
    full = pl.BlockSpec(memory_space=pltpu.VMEM)
    any_place = pl.BlockSpec(memory_space=pl.ANY)
    units = query.shape[1] // head_width
    return pl.pallas_call(
        functools.partial(attention_kernel, start, group),
        out_shape=jax.ShapeDtypeStruct(query.shape, jnp.bfloat16),
        in_specs=[pl.BlockSpec(memory_space=pltpu.SMEM), full, any_place, any_place, any_place],
        out_specs=full,
        scratch_shapes=[
            pltpu.VMEM((kv_local, count, head_width), jnp.bfloat16),
            pltpu.VMEM((kv_local, count, 2 * head_width), jnp.bfloat16),
            pltpu.VMEM((rows, count), jnp.float32),
            pltpu.VMEM((rows, count), jnp.float32),
            pltpu.VMEM((rows, head_width), jnp.float32),
            pltpu.VMEM((rows, count), jnp.bfloat16),
            pltpu.VMEM((rows, count), jnp.bfloat16),
            pltpu.VMEM((rows, 2 * head_width), jnp.float32),
            pltpu.SemaphoreType.DMA((kv_local * 2 * (picked + 1),)),
        ],
        compiler_params=pltpu.CompilerParams(vmem_limit_bytes=48 * 1024 * 1024),
        cost_estimate=pl.CostEstimate(
            flops=8 * rows * count * head_width * units, transcendentals=rows * count * units,
            bytes_accessed=4 * kv_local * count * head_width),
        name=f"attend_{start}",
    )(owners, query, own_keys, own_values, got)


CHUNKS = 2


def shards(queries, own_keys, own_values, cache_keys, cache_values, selected, out_weight):
    block_rows = queries.shape[0]
    kv_local, _, head_width = cache_keys.shape
    blocks_dev = cache_keys.shape[1] // block_rows
    group = queries.shape[1] // kv_local
    picked = selected[0]
    owners = picked // blocks_dev
    owner_count = lax.axis_size("ctx")
    match = owners[:, :, None] == jnp.arange(owner_count, dtype=jnp.int32)[None, None, :]
    request = jnp.sum(jnp.where(match, (picked % blocks_dev)[:, :, None], 0), axis=1).T
    wanted = lax.all_to_all(request, "ctx", split_axis=0, concat_axis=0, tiled=True)
    heads = jnp.arange(kv_local, dtype=jnp.int32)[None, :]
    shape = (kv_local, blocks_dev, block_rows, head_width)
    sent = jnp.stack([cache_keys.reshape(shape)[heads, wanted], cache_values.reshape(shape)[heads, wanted]], axis=2)
    got = lax.all_to_all(sent, "ctx", split_axis=0, concat_axis=0, tiled=True)
    query = queries.reshape(block_rows, -1)
    keys = jnp.transpose(own_keys, (1, 0, 2))
    values = jnp.transpose(own_values, (1, 0, 2))
    rows = block_rows // CHUNKS
    outputs = []
    for start in range(0, block_rows, rows):
        attended = attend(start, group, owners, query[start:start + rows], keys, values, got)
        term = jnp.dot(attended, out_weight, preferred_element_type=jnp.float32).astype(jnp.bfloat16)
        outputs.append(lax.psum_scatter(term, "tp", scatter_dimension=1, tiled=True))
    return jnp.concatenate(outputs, axis=0)


def solution(mesh):
    in_specs = (
        P("ctx", "tp", None),
        P("ctx", "tp", None),
        P("ctx", "tp", None),
        P("tp", "ctx", None),
        P("tp", "ctx", None),
        P("ctx", "tp", None),
        P("tp", None),
    )
    return jax.shard_map(shards, mesh=mesh, in_specs=in_specs, out_specs=P("ctx", "tp"), check_vma=False)
```

time: 542 us -> 295 us (0.54)
  other arithmetic: 159 us -> 7.96 us
  matrix products: 129 us -> 33 us
  Pallas kernels: 0 us -> 60.1 us
  local copies, waits for them, and re-layouts: 36.7 us -> 8.95 us
  waiting for transfers between devices: 181 us -> 156 us
    sub x9 -> x0, other arithmetic: 128 us -> none  [the longest x8 128 us: one_pair(): powers = jnp.exp(scores - largest)]
    dot_general x16 -> x0, matrix products: 103 us -> none  [the longest x8 74.3 us: one_pair(): jnp.einsum('gtk,kd->gtd', weights, value_set, preferred_element_type=jnp....]
    pallas_call x0 -> x2, Pallas kernels: none -> 60.1 us  [attend(): pl.pallas_call(functools.partial(attention_kernel, start, group), out_sha...]
    reduce_scatter x1 -> x2, waiting for transfers between devices: 144 us -> 109 us  [shards(): lax.psum_scatter(term, 'tp', scatter_dimension=1, tiled=True)]
    or x8 -> x0, other arithmetic: 24.2 us -> none  [attend(): allowed = (column < remote_count) | (column - remote_count <= row_index)]
    all_to_all x2 -> x1, waiting for transfers between devices: 37 us -> 46.7 us  [shards(): got = lax.all_to_all(sent, 'ctx', split_axis=0, concat_axis=0, tiled=True)]
    gather x6 -> x2, local copies, waits for them, and re-layouts: 13.6 us -> 6.02 us  [the longest x1 3.88 us: shards(): cache_keys.reshape(shape)[heads, wanted]]
    dot_general x1 -> x2, matrix products: 26 us -> 33 us  [shards(): jnp.dot(attended, out_weight, preferred_element_type=jnp.float32)]
  transfers between devices with their start and end apart: 3 -> 3, of which waited for: 3 -> 3; matrix products, arithmetic and copies ran while one was open for 3% -> 7% of each run, Pallas kernels for 0% -> 10%
where the time goes in v1:
time: 295 us; the launch traced here: 294 us
  waiting for transfers between devices  156 us (53%)
  Pallas kernels  60.1 us (20%)
  matrix products  33 us (11%)
  between operations  13.5 us (5%)
  blocking collectives  9.67 us (3%)
  local copies, waits for them, and re-layouts  8.95 us (3%)
  other arithmetic  7.96 us (3%)
  starting transfers between devices  4.82 us (2%)
    reduce_scatter x2, waiting for transfers between devices, shards(): lax.psum_scatter(term, 'tp', scatter_dimension=1, tiled=True)  109 us
    pallas_call x2, Pallas kernels, attend(): pl.pallas_call(functools.partial(attention_kernel, start, group), out_sha...  60.1 us
    all_to_all x1, waiting for transfers between devices, shards(): got = lax.all_to_all(sent, 'ctx', split_axis=0, concat_axis=0, tiled=True)  46.7 us
    dot_general x2, matrix products, shards(): jnp.dot(attended, out_weight, preferred_element_type=jnp.float32)  33 us
    all_to_all x1, blocking collectives, shards(): lax.all_to_all(request, 'ctx', split_axis=0, concat_axis=0, tiled=True)  9.67 us
  transfers between devices with their start and end apart: 3, of which 3 were waited for; matrix products, arithmetic and copies ran while one was open for 7% of the time, Pallas kernels for 10%

profile of v1, /device:TPU:0, one launch (start us, length us, event | category | flops | bytes accessed | tf_op | source)
XLA Modules:
  0.0 294.2 jit_solution(16789696769151842624)
XLA Ops:
  6.5 0.0 copy-start
  6.5 0.8 and_select_fusion
  7.4 0.1 select_reduce_fusion
  7.5 0.1 copy.21
  7.5 9.7 %all_to_all.17 = s32[8,1,2]{2,1,0:T(1,128)S(1)} all-to-all(s32[8,1,2]{2,1,0:T(1,128)S(1)} %copy.21), channel_id=1, replica_groups=mesh['ctx'=8,'tp'=4] {'ctx'}, dimensions={0} | all-to-all | bytes 128 | tf_op jit(solution)/shard_map/all_to_all | solution.py:149
  17.2 0.1 copy.22
  17.3 0.1 copy.23
  17.4 0.1 reshape.93
  17.5 0.0 copy-done
  17.5 2.1 gather_fusion.1
  19.6 0.0 copy-start.2
  19.6 3.9 %gather_fusion = bf16[16,512,128]{2,1,0:T(8,128)(2,1)} fusion(bf16[2,8,512,128]{3,2,1,0:T(8,128)(2,1)} %bitcast.54, s32[16]{0:T(128)S(1)} %reshape.93), kind=kCustom, calls=%fused_computation | custom fusion | bytes 4194432 | tf_op jit(solution)/shard_map/gather | solution.py:152
  23.5 0.0 copy-done.2
  23.5 3.9 %pad_maximum_fusion = bf16[8,2,2,512,128]{4,3,2,1,0:T(8,128)(2,1)} fusion(bf16[8,2,1,512,128]{4,3,2,1,0:T(8,128)(2,1)S(1)} %bitcast.50, bf16[8,2,1,512,128]{4,3,2,1,0:T(8,128)(2,1)} %bitcast.51), kind=kLoop, calls=%fused_computation.4 | loop fusion | flops 2097152 | bytes 8388608 | tf_op jit(solution)/shard_map/stack | solution.py:152
  27.4 4.6 %all-to-all-start.1 = ((bf16[8,2,2,512,128]{4,3,2,1,0:T(8,128)(2,1)}), bf16[8,2,2,512,128]{4,3,2,1,0:T(8,128)(2,1)}, u32[]{:S(2)}, u32[]{:S(2)}) async-start(bf16[8,2,2,512,128]{4,3,2,1,0:T(8,128)(2,1)} %pad_maximum_fusion), calls=%async_computation.1 | async-start | bytes 8388608 | tf_op jit(solution)/shard_map/all_to_all | solution.py:153
  32.0 0.0 copy-start.3
  32.0 0.0 reduce-scatter.5.cloned.1.call-start
  32.1 0.0 copy-start.4
  32.1 1.9 fusion.3
  34.0 0.3 copy.30
  34.3 0.0 copy-done.3
  34.3 0.0 copy-done.4
  34.3 0.1 copy_bitcast_fusion.2
  34.4 46.7 %all-to-all-done.1.got = bf16[8,2,2,512,128]{4,3,2,1,0:T(8,128)(2,1)} async-done(((bf16[8,2,2,512,128]{4,3,2,1,0:T(8,128)(2,1)}), bf16[8,2,2,512,128]{4,3,2,1,0:T(8,128)(2,1)}, u32[]{:S(2)}, u32[]{:S(2)}) %all-to-all-start.1) | async-done | bytes 4194336 | tf_op jit(solution)/shard_map/all_to_all | solution.py:153
  81.1 30.7 %attend_256.1 = bf16[256,2048]{1,0:T(8,128)(2,1)S(1)} custom-call(s32[2,8]{1,0:T(2,128)S(1)} %get-tuple-element.8.owner_ref, bf16[256,2048]{1,0:T(8,128)(2,1)S(1)} %bitcast.48, bf16[2,512,128]{2,1,0:T(8,128)(2,1)S(1)} %get-tuple-element.10.own_keys, bf16[2,512,128]{2,1,0:T(8,128)(2,1)S(1)} %get-tuple-element.9.own_values, ...), custom_call_target="tpu_custom_call" | custom-call | flops 19327352832 | bytes 4718592 | tf_op jit(solution)/shard_map/attend_256/pallas_call | solution.py:112
  111.8 16.4 %convolution_convert_fusion = bf16[256,8192]{1,0:T(8,128)(2,1)} fusion(bf16[256,2048]{1,0:T(8,128)(2,1)S(1)} %attend_256.1, bf16[2048,8192]{1,0:T(8,128)(2,1)} %param.13), kind=kOutput, calls=%fused_computation.2 | convolution fusion | flops 8592031744 | bytes 38797312 | tf_op jit(solution)/shard_map/dot_general | solution.py:161
  128.2 0.0 reduce-scatter.5.cloned.1.call-update
  128.2 0.2 reduce-scatter.3.cloned.1.call-start
  128.5 0.3 copy.31
  128.8 29.4 %attend_0.1 = bf16[256,2048]{1,0:T(8,128)(2,1)S(1)} custom-call(s32[2,8]{1,0:T(2,128)S(1)} %get-tuple-element.8.owner_ref, bf16[256,2048]{1,0:T(8,128)(2,1)S(1)} %bitcast.49, bf16[2,512,128]{2,1,0:T(8,128)(2,1)S(1)} %get-tuple-element.10.own_keys, bf16[2,512,128]{2,1,0:T(8,128)(2,1)S(1)} %get-tuple-element.9.own_values, ...), custom_call_target="tpu_custom_call" | custom-call | flops 18253611008 | bytes 4456448 | tf_op jit(solution)/shard_map/attend_0/pallas_call | solution.py:112
  158.2 16.6 %convolution_convert_fusion.1 = bf16[256,8192]{1,0:T(8,128)(2,1)} fusion(bf16[256,2048]{1,0:T(8,128)(2,1)S(1)} %attend_0.1, bf16[2048,8192]{1,0:T(8,128)(2,1)} %param.13), kind=kOutput, calls=%fused_computation.3 | convolution fusion | flops 8592031744 | bytes 38797312 | tf_op jit(solution)/shard_map/dot_general | solution.py:161
  174.8 0.0 copy-start.1
  174.8 0.0 reduce-scatter.3.cloned.1.call-update
  174.8 29.8 %reduce-scatter.5.cloned.1.call-done = bf16[256,2048]{1,0:T(8,128)(2,1)} async-done(((bf16[256,8192]{1,0:T(8,128)(2,1)}), bf16[256,2048]{1,0:T(8,128)(2,1)}) %reduce-scatter.5.cloned.1.call-update) | async-done | bytes 1048592 | tf_op jit(solution)/shard_map/reduce_scatter | solution.py:162
  204.6 79.6 %reduce-scatter.3.cloned.1.call-done = bf16[256,2048]{1,0:T(8,128)(2,1)} async-done(((bf16[256,8192]{1,0:T(8,128)(2,1)}), bf16[256,2048]{1,0:T(8,128)(2,1)}) %reduce-scatter.3.cloned.1.call-update) | async-done | bytes 1048592 | tf_op jit(solution)/shard_map/reduce_scatter | solution.py:162
  284.2 3.1 %pad_maximum_fusion.1 = bf16[512,2048]{1,0:T(8,128)(2,1)} fusion(bf16[256,2048]{1,0:T(8,128)(2,1)} %reduce-scatter.5.cloned.1.call-done, bf16[256,2048]{1,0:T(8,128)(2,1)} %reduce-scatter.3.cloned.1.call-done), kind=kLoop, calls=%fused_computation.5 | loop fusion | flops 4194304 | bytes 4194304 | tf_op jit(solution)/shard_map/concatenate | solution.py:163
  287.3 0.0 copy-done.1
  (1 shorter events, 0.0 us)
Async XLA Ops:
  6.5 10.9 %copy-start = (bf16[2,4096,128]{2,1,0:T(8,128)(2,1)S(1)}, bf16[2,4096,128]{2,1,0:T(8,128)(2,1)}, u32[]{:S(2)}) copy-start(bf16[2,4096,128]{2,1,0:T(8,128)(2,1)} %param.11) | copy-start | bytes 6291460
  19.6 3.9 %copy-start.2 = (bf16[16,512,128]{2,1,0:T(8,128)(2,1)S(1)}, bf16[16,512,128]{2,1,0:T(8,128)(2,1)}, u32[]{:S(2)}) copy-start(bf16[16,512,128]{2,1,0:T(8,128)(2,1)} %gather_fusion.1) | copy-start | bytes 6291460
  27.4 53.7 %all-to-all-start.1 = ((bf16[8,2,2,512,128]{4,3,2,1,0:T(8,128)(2,1)}), bf16[8,2,2,512,128]{4,3,2,1,0:T(8,128)(2,1)}, u32[]{:S(2)}, u32[]{:S(2)}) async-start(bf16[8,2,2,512,128]{4,3,2,1,0:T(8,128)(2,1)} %pad_maximum_fusion), calls=%async_computation.1 | async-start | bytes 8388608 | tf_op jit(solution)/shard_map/all_to_all | solution.py:153
  32.0 2.3 copy-start.3
  32.0 172.6 %reduce-scatter.5.cloned.1.call-start = ((), (), s32[]{:S(2)}) async-start(), calls=%async_computation.5 | async-start | bytes 5242880 | tf_op jit(solution)/shard_map/reduce_scatter | solution.py:162
  32.1 2.3 copy-start.4
  128.2 156.0 %reduce-scatter.3.cloned.1.call-start = ((), (), s32[]{:S(2)}) async-start(), calls=%async_computation.4 | async-start | bytes 5242880 | tf_op jit(solution)/shard_map/reduce_scatter | solution.py:162
  174.8 112.6 %copy-start.1 = (bf16[2,4096,128]{2,1,0:T(8,128)(2,1)S(1)}, bf16[2,4096,128]{2,1,0:T(8,128)(2,1)}, u32[]{:S(2)}) copy-start(bf16[2,4096,128]{2,1,0:T(8,128)(2,1)} %param.11) | copy-start | bytes 6291460
Sparse Core Ops, SparseCore 0:
  128.4 76.1 reduce-scatter.4
  206.9 77.2 reduce-scatter.2

commit v2 on v1

v2 whole, which is shorter than its diff:
```python
import functools

import jax
import jax.numpy as jnp
from jax import lax
from jax.experimental import pallas as pl
from jax.experimental.pallas import tpu as pltpu
from jax.sharding import PartitionSpec as P

LOG2E = 1.4426950408889634


def gather_kernel(wanted_ref, keys_ref, values_ref, out_ref):
    out_ref[0, 0] = keys_ref[0]
    out_ref[0, 1] = values_ref[0]


def gather(head, wanted, cache_keys, cache_values, block):
    count = wanted.shape[0]
    head_width = cache_keys.shape[2]
    spec = pl.BlockSpec((1, block, head_width), lambda owner, ids: (head, ids[owner, head], 0))
    return pl.pallas_call(
        gather_kernel,
        out_shape=jax.ShapeDtypeStruct((count, 2, block, head_width), cache_keys.dtype),
        grid_spec=pltpu.PrefetchScalarGridSpec(
            num_scalar_prefetch=1, grid=(count,), in_specs=[spec, spec],
            out_specs=pl.BlockSpec((1, 2, block, head_width), lambda owner, ids: (owner, 0, 0, 0))),
        compiler_params=pltpu.CompilerParams(vmem_limit_bytes=60 * 1024 * 1024),
        name=f"gather_{head}",
    )(wanted, cache_keys, cache_values)


def fused_kernel(start, rows, tile, owner_ref, query_ref, own_keys, own_values, got, earlier, weight, term_ref,
                 held, mine, weight_sem, *scratch):
    copy = pltpu.make_async_copy(weight, held, weight_sem)
    attention_kernel(start, rows, owner_ref, query_ref, own_keys, own_values, got, mine, *scratch, copy=copy)
    copy.wait()
    depth = earlier.shape[1]

    def column(index, carry):
        place = pl.ds(pl.multiple_of(index * tile, tile), tile)
        term = jnp.dot(mine[...], held[depth:, place], preferred_element_type=jnp.float32)
        if depth:
            term += jnp.dot(earlier[...], held[:depth, place], preferred_element_type=jnp.float32)
        term_ref[:, place] = term.astype(term_ref.dtype)
        return carry

    lax.fori_loop(0, weight.shape[1] // tile, column, 0)


def attention_kernel(start, rows, owner_ref, query_ref, own_keys, own_values, got, out_ref,
                     keys, values, scores_a, scores_b, peaks, powers_a, powers_b, total, sems, copy=None):
    all_rows, width = query_ref.shape
    head_width = own_keys.shape[-1]
    picked = owner_ref.shape[0]
    block = got.shape[2]
    stop = start + all_rows
    cached = picked * block
    group = width // head_width
    units = group * (all_rows // rows)
    factor = head_width ** -0.5 * LOG2E

    copies = []
    for slot in range(picked):
        place = pl.ds(slot * block, block)
        owner = owner_ref[slot]
        copies.append(pltpu.make_async_copy(got.at[owner, 0], keys.at[place], sems.at[len(copies)]))
        copies.append(pltpu.make_async_copy(
            got.at[owner, 1], values.at[place, pl.ds(0, head_width)], sems.at[len(copies)]))
    place = pl.ds(cached, stop)
    copies.append(pltpu.make_async_copy(own_keys.at[pl.ds(0, stop)], keys.at[place], sems.at[len(copies)]))
    copies.append(pltpu.make_async_copy(
        own_values.at[pl.ds(0, stop)], values.at[place, pl.ds(0, head_width)], sems.at[len(copies)]))
    for item in copies:
        item.start()
    values[:, head_width:] = jnp.ones((cached + stop, head_width), jnp.bfloat16)
    for item in copies:
        item.wait()
    if copy is not None:
        copy.start()

    step = 2 * block
    cuts = [(first, min(step, cached - first)) for first in range(0, cached, step)] + [(cached, stop)]

    def place_of(unit):
        row = pl.multiple_of(unit // group * rows, rows)
        return row, (pl.ds(row, rows), pl.ds(pl.multiple_of(unit % group * head_width, head_width), head_width))

    def phase(unit, scores_now, scores_next, powers_now, powers_before, stages=(True, True, True)):
        ahead, middle, last = stages
        if ahead:
            first_row, place = place_of(unit + 1)
            query = query_ref[place]
        if middle:
            peak = peaks[...]
        lanes = None
        for index, (first, size) in enumerate(cuts):
            if ahead:
                part = lax.dot_general(query, keys[first:first + size], (((1,), (1,)), ((), ())),
                                       preferred_element_type=jnp.float32)
                if first == cached:
                    row = lax.broadcasted_iota(jnp.int32, part.shape, 0)
                    column = lax.broadcasted_iota(jnp.int32, part.shape, 1)
                    part = jnp.where(column <= row + (first_row + start), part, -jnp.inf)
                scores_next[:, first:first + size] = part
                for lane in range(0, size, head_width):
                    piece = part[:, lane:lane + head_width]
                    lanes = piece if lanes is None else jnp.maximum(lanes, piece)
            if middle:
                for lane in range(first, first + size, head_width):
                    powers_now[:, lane:lane + head_width] = jnp.exp2(
                        (scores_now[:, lane:lane + head_width] - peak) * factor).astype(jnp.bfloat16)
            if last:
                term = jnp.dot(powers_before[:, first:first + size], values[first:first + size],
                               preferred_element_type=jnp.float32)
                if index == 0:
                    total[...] = term
                elif index < len(cuts) - 1:
                    total[...] += term
                else:
                    term = total[...] + term
                    out_ref[place_of(unit - 1)[1]] = (
                        term[:, :head_width] / term[:, head_width:]).astype(jnp.bfloat16)
        if ahead:
            peaks[...] = jnp.broadcast_to(jnp.max(lanes, axis=1, keepdims=True), peaks.shape)

    phase(-1, scores_a, scores_b, powers_a, powers_b, (True, False, False))
    phase(0, scores_b, scores_a, powers_b, powers_a, (True, True, False))

    def pair(index, carry):
        phase(2 * index + 1, scores_a, scores_b, powers_a, powers_b)
        phase(2 * index + 2, scores_b, scores_a, powers_b, powers_a)
        return carry

    lax.fori_loop(0, units // 2 - 1, pair, 0)
    phase(units - 1, scores_a, scores_b, powers_a, powers_b, (False, True, True))
    phase(units, scores_b, scores_a, powers_b, powers_a, (False, False, True))


def attend(name, start, rows, owners, query, own_keys, own_values, got, earlier=None, weight=None):
    all_rows, width = query.shape
    head_width = own_keys.shape[-1]
    picked = owners.shape[0]
    count = picked * got.shape[2] + start + all_rows
    full = pl.BlockSpec(memory_space=pltpu.VMEM)
    any_place = pl.BlockSpec(memory_space=pl.ANY)
    heads = width // head_width
    scratch = [
        pltpu.VMEM((count, head_width), jnp.bfloat16),
        pltpu.VMEM((count, 2 * head_width), jnp.bfloat16),
        pltpu.VMEM((rows, count), jnp.float32),
        pltpu.VMEM((rows, count), jnp.float32),
        pltpu.VMEM((rows, head_width), jnp.float32),
        pltpu.VMEM((rows, count), jnp.bfloat16),
        pltpu.VMEM((rows, count), jnp.bfloat16),
        pltpu.VMEM((rows, 2 * head_width), jnp.float32),
        pltpu.SemaphoreType.DMA((2 * (picked + 1),)),
    ]
    specs = [pl.BlockSpec(memory_space=pltpu.SMEM), full, any_place, any_place, any_place]
    operands = [owners, query, own_keys, own_values, got]
    flops = 8 * all_rows * count * head_width * heads
    moved = 4 * count * head_width
    limit = 40
    if weight is None:
        kernel = functools.partial(attention_kernel, start, rows)
        shape = query.shape
    else:
        kernel = functools.partial(fused_kernel, start, rows, 512)
        shape = (all_rows, weight.shape[1])
        scratch = [pltpu.VMEM(weight.shape, weight.dtype), pltpu.VMEM(query.shape, jnp.bfloat16),
                   pltpu.SemaphoreType.DMA] + scratch
        specs = specs + [full, any_place]
        operands = operands + [earlier, weight]
        flops += 2 * all_rows * weight.shape[0] * weight.shape[1]
        moved += 2 * weight.shape[0] * weight.shape[1]
        limit = 60
    return pl.pallas_call(
        kernel,
        out_shape=jax.ShapeDtypeStruct(shape, jnp.bfloat16),
        in_specs=specs,
        out_specs=full,
        scratch_shapes=scratch,
        compiler_params=pltpu.CompilerParams(vmem_limit_bytes=limit * 1024 * 1024),
        cost_estimate=pl.CostEstimate(
            flops=flops, transcendentals=all_rows * count * heads, bytes_accessed=moved),
        name=name,
    )(*operands)


def shards(queries, own_keys, own_values, cache_keys, cache_values, selected, out_weight):
    block_rows = queries.shape[0]
    kv_local, _, head_width = cache_keys.shape
    blocks_dev = cache_keys.shape[1] // block_rows
    group_width = queries.shape[1] // kv_local * head_width
    picked = selected[0]
    owners = picked // blocks_dev
    owner_count = lax.axis_size("ctx")
    match = owners[:, :, None] == jnp.arange(owner_count, dtype=jnp.int32)[None, None, :]
    request = jnp.sum(jnp.where(match, (picked % blocks_dev)[:, :, None], 0), axis=1).T
    wanted = lax.all_to_all(request, "ctx", split_axis=0, concat_axis=0, tiled=True)
    got = []
    for head in range(kv_local):
        sent = gather(head, wanted, cache_keys, cache_values, block_rows)
        if got:
            sent, got[-1] = lax.optimization_barrier((sent, got[-1]))
        got.append(lax.all_to_all(sent, "ctx", split_axis=0, concat_axis=0, tiled=True))
    query = queries.reshape(block_rows, -1)
    keys = jnp.transpose(own_keys, (1, 0, 2))
    values = jnp.transpose(own_values, (1, 0, 2))

    def part(head, start, stop, rows, *more):
        return attend(f"attend_{head}_{start}", start, rows, owners[head],
                      query[start:stop, head * group_width:(head + 1) * group_width],
                      keys[head], values[head], got[head], *more)

    last = kv_local - 1
    short = block_rows // 4
    rest = (block_rows - short) // 2
    most = block_rows - short
    if last:
        first = [part(head, 0, most, rest) for head in range(last)]
        term = part(last, 0, short, short, jnp.concatenate([item[:short] for item in first], axis=1), out_weight)
        term, query = lax.optimization_barrier((term, query))
        whole = [jnp.concatenate([first[head][short:], part(head, most, block_rows, short)], axis=0)
                 for head in range(last)]
    else:
        attended = part(last, 0, short, short)
        term = jnp.dot(attended, out_weight, preferred_element_type=jnp.float32).astype(jnp.bfloat16)
        term, query = lax.optimization_barrier((term, query))
        whole = []
    outputs = [lax.psum_scatter(term, "tp", scatter_dimension=1, tiled=True)]
    attended = jnp.concatenate(whole + [part(last, short, block_rows, rest)], axis=1)
    term = jnp.dot(attended, out_weight, preferred_element_type=jnp.float32).astype(jnp.bfloat16)
    outputs.append(lax.psum_scatter(term, "tp", scatter_dimension=1, tiled=True))
    return jnp.concatenate(outputs, axis=0)


def solution(mesh):
    in_specs = (
        P("ctx", "tp", None),
        P("ctx", "tp", None),
        P("ctx", "tp", None),
        P("tp", "ctx", None),
        P("tp", "ctx", None),
        P("ctx", "tp", None),
        P("tp", None),
    )
    return jax.shard_map(shards, mesh=mesh, in_specs=in_specs, out_specs=P("ctx", "tp"), check_vma=False)
```

time: 295 us -> 292 us (0.990)
  Pallas kernels: 60.1 us -> 90.5 us
  waiting for transfers between devices: 156 us -> 133 us
  matrix products: 33 us -> 21.1 us
  other arithmetic: 7.96 us -> 3.86 us
    pallas_call x2 -> x6, Pallas kernels: 60.1 us -> 90.5 us  [the longest x4 77.9 us: attend(): pl.pallas_call(kernel, out_shape=jax.ShapeDtypeStruct(shape, jnp.bfloat16...]
    all_to_all x1 -> x2, waiting for transfers between devices: 46.7 us -> 20 us  [shards(): lax.all_to_all(sent, 'ctx', split_axis=0, concat_axis=0, tiled=True)]
    dot_general x2 -> x1, matrix products: 33 us -> 21.1 us  [shards(): jnp.dot(attended, out_weight, preferred_element_type=jnp.float32)]
    gather x2 -> x0, local copies, waits for them, and re-layouts: 6.02 us -> none  [the longest x1 3.88 us: shards(): cache_keys.reshape(shape)[heads, wanted]]
    unnamed x12 -> x27, local copies, waits for them, and re-layouts: 0.57 us -> 5.75 us
    another operation x1 -> x0, other arithmetic: 3.92 us -> none  [shards(): jnp.stack([cache_keys.reshape(shape)[heads, wanted], cache_values.reshape...]
    reduce_scatter x2 -> x1, waiting for transfers between devices: 109 us -> 113 us  [shards(): lax.psum_scatter(term, 'tp', scatter_dimension=1, tiled=True)]
    all_to_all x1 -> x2, starting transfers between devices: 4.56 us -> 7.21 us  [shards(): lax.all_to_all(sent, 'ctx', split_axis=0, concat_axis=0, tiled=True)]
  transfers between devices with their start and end apart: 3 -> 4, of which waited for: 3 -> 2; matrix products, arithmetic and copies ran while one was open for 7% -> 10% of each run, Pallas kernels for 10% -> 21%
where the time goes in v2:
time: 292 us; the launch traced here: 291 us
  waiting for transfers between devices  133 us (46%)
  Pallas kernels  90.5 us (31%)
  matrix products  21.1 us (7%)
  between operations  13.6 us (5%)
  local copies, waits for them, and re-layouts  11.8 us (4%)
  blocking collectives  9.67 us (3%)
  starting transfers between devices  7.47 us (3%)
  other arithmetic  3.86 us (1%)
    reduce_scatter x1, waiting for transfers between devices, shards(): lax.psum_scatter(term, 'tp', scatter_dimension=1, tiled=True)  113 us
    pallas_call x4, Pallas kernels, attend(): pl.pallas_call(kernel, out_shape=jax.ShapeDtypeStruct(shape, jnp.bfloat16...  77.9 us
    dot_general x1, matrix products, shards(): jnp.dot(attended, out_weight, preferred_element_type=jnp.float32)  21.1 us
    all_to_all x2, waiting for transfers between devices, shards(): lax.all_to_all(sent, 'ctx', split_axis=0, concat_axis=0, tiled=True)  20 us
    pallas_call x2, Pallas kernels, gather(): pl.pallas_call(gather_kernel, out_shape=jax.ShapeDtypeStruct((count, 2, b...  12.6 us
    all_to_all x1, blocking collectives, shards(): lax.all_to_all(request, 'ctx', split_axis=0, concat_axis=0, tiled=True)  9.67 us
    all_to_all x2, starting transfers between devices, shards(): lax.all_to_all(sent, 'ctx', split_axis=0, concat_axis=0, tiled=True)  7.21 us
  transfers between devices with their start and end apart: 4, of which 2 were waited for; matrix products, arithmetic and copies ran while one was open for 10% of the time, Pallas kernels for 21%

profile of v2, /device:TPU:0, one launch (start us, length us, event | category | flops | bytes accessed | tf_op | source)
XLA Modules:
  0.0 290.7 jit_solution(205477199660027368)
XLA Ops:
  6.5 0.7 and_select_fusion
  7.2 0.1 select_reduce_fusion
  7.3 0.1 copy.20
  7.4 9.7 %all_to_all.21 = s32[8,1,2]{2,1,0:T(1,128)S(1)} all-to-all(s32[8,1,2]{2,1,0:T(1,128)S(1)} %copy.20), channel_id=1, replica_groups=mesh['ctx'=8,'tp'=4] {'ctx'}, dimensions={0} | all-to-all | bytes 128 | tf_op jit(solution)/shard_map/all_to_all | solution.py:200
  17.1 0.1 copy.21
  17.2 0.7 copy.22.wanted_ref
  17.8 6.1 %gather_0.1 = bf16[8,2,512,128]{3,2,1,0:T(8,128)(2,1)} custom-call(s32[8,2]{1,0:T(8,128)} %copy.22.wanted_ref, bf16[2,4096,128]{2,1,0:T(8,128)(2,1)} %keys_ref.3, bf16[2,4096,128]{2,1,0:T(8,128)(2,1)} %values_ref.3), custom_call_target="tpu_custom_call" | custom-call | tf_op jit(solution)/shard_map/gather_0/pallas_call | solution.py:22
  23.9 3.6 %all-to-all-start.1 = ((bf16[8,2,512,128]{3,2,1,0:T(8,128)(2,1)}), bf16[8,2,512,128]{3,2,1,0:T(8,128)(2,1)S(1)}, u32[]{:S(2)}, u32[]{:S(2)}) async-start(bf16[8,2,512,128]{3,2,1,0:T(8,128)(2,1)} %gather_0.1), calls=%async_computation.1 | async-start | bytes 4194304 | tf_op jit(solution)/shard_map/all_to_all | solution.py:206
  27.5 6.6 %gather_1.1 = bf16[8,2,512,128]{3,2,1,0:T(8,128)(2,1)} custom-call(s32[8,2]{1,0:T(8,128)} %copy.22.wanted_ref, bf16[2,4096,128]{2,1,0:T(8,128)(2,1)} %keys_ref.3, bf16[2,4096,128]{2,1,0:T(8,128)(2,1)} %values_ref.3), custom_call_target="tpu_custom_call" | custom-call | tf_op jit(solution)/shard_map/gather_1/pallas_call | solution.py:22
  34.1 20.0 %all-to-all-done.1.got = bf16[8,2,512,128]{3,2,1,0:T(8,128)(2,1)S(1)} async-done(((bf16[8,2,512,128]{3,2,1,0:T(8,128)(2,1)}), bf16[8,2,512,128]{3,2,1,0:T(8,128)(2,1)S(1)}, u32[]{:S(2)}, u32[]{:S(2)}) %all-to-all-start.1) | async-done | bytes 2097184 | tf_op jit(solution)/shard_map/all_to_all | solution.py:206
  54.0 1.3 copy-done.2
  55.4 3.6 %all-to-all-start.2 = ((bf16[8,2,512,128]{3,2,1,0:T(8,128)(2,1)}), bf16[8,2,512,128]{3,2,1,0:T(8,128)(2,1)S(1)}, u32[]{:S(2)}, u32[]{:S(2)}) async-start(bf16[8,2,512,128]{3,2,1,0:T(8,128)(2,1)} %gather_1.1), calls=%async_computation.2 | async-start | bytes 4194304 | tf_op jit(solution)/shard_map/all_to_all | solution.py:206
  59.0 0.0 reduce-scatter.3.cloned.1.call-start
  59.0 2.1 copy.28
  61.2 0.0 copy-start.9
  61.2 0.0 copy-start.10
  61.2 0.0 copy-start.11
  61.2 0.0 copy-start.3
  61.2 0.7 slice.54.query_ref
  62.0 0.1 slice.57.query_ref
  62.0 0.3 copy-done.10
  62.4 0.2 copy-done.11
  62.6 0.6 slice_bitcast_fusion.4
  63.2 0.8 slice_bitcast_fusion
  64.0 22.5 %attend_0_0.1 = bf16[384,1024]{1,0:T(8,128)(2,1)S(1)} custom-call(s32[8]{0:T(128)S(1)} %get-tuple-element.17.owner_ref, bf16[384,1024]{1,0:T(8,128)(2,1)S(1)} %slice.57.query_ref, bf16[512,128]{1,0:T(8,128)(2,1)S(1)} %get-tuple-element.22.own_keys, bf16[512,128]{1,0:T(8,128)(2,1)S(1)} %get-tuple-element.13.own_values, bf16[8,2,512,128]{3,2,1,0:T(8,128)(2,1)S(1)} %copy-done.3), custom_call_target="tpu_custom_call" | custom-call | flops 14092861440 | bytes 2293760 | tf_op jit(solution)/shard_map/attend_0_0/pallas_call | solution.py:177
  86.5 0.8 slice.60.earlier
  87.3 0.0 all-to-all-done.2.got
  87.3 1.3 copy-done
  88.6 22.1 %attend_1_0.1 = bf16[128,8192]{1,0:T(8,128)(2,1)} custom-call(s32[8]{0:T(128)} %get-tuple-element.18.owner_ref, bf16[128,1024]{1,0:T(8,128)(2,1)} %slice.54.query_ref, bf16[512,128]{1,0:T(8,128)(2,1)} %get-tuple-element.21.own_keys, bf16[512,128]{1,0:T(8,128)(2,1)} %get-tuple-element.14.own_values, bf16[8,2,512,128]{3,2,1,0:T(8,128)(2,1)} %copy-done, ...), custom_call_target="tpu_custom_call" | custom-call | flops 8724152320 | bytes 35717120 | tf_op jit(solution)/shard_map/attend_1_0/pallas_call | solution.py:177
  110.7 0.0 copy-done.5
  110.7 0.0 copy-start.4
  110.7 0.0 reduce-scatter.3.cloned.1.call-update
  110.8 0.2 reduce-scatter.5.cloned.1.call-start
  111.0 1.1 slice.52.query_ref
  112.1 0.3 copy-done.4
  112.4 10.0 %attend_0_384.1 = bf16[128,1024]{1,0:T(8,128)(2,1)S(1)} custom-call(s32[8]{0:T(128)S(1)} %get-tuple-element.17.owner_ref, bf16[128,1024]{1,0:T(8,128)(2,1)S(1)} %slice.52.query_ref, bf16[512,128]{1,0:T(8,128)(2,1)S(1)} %get-tuple-element.22.own_keys, bf16[512,128]{1,0:T(8,128)(2,1)S(1)} %get-tuple-element.13.own_values, bf16[8,2,512,128]{3,2,1,0:T(8,128)(2,1)S(1)} %copy-done.4), custom_call_target="tpu_custom_call" | custom-call | flops 4831838208 | bytes 2359296 | tf_op jit(solution)/shard_map/attend_0_384/pallas_call | solution.py:177
  122.4 1.2 slice.53.query_ref
  123.6 0.0 copy-done.1
  123.6 0.0 copy-done.6
  123.7 0.0 copy-done.7
  123.7 0.0 copy-done.8
  123.7 0.0 slice-start
  123.7 23.3 %attend_1_128.1 = bf16[384,1024]{1,0:T(8,128)(2,1)S(1)} custom-call(s32[8]{0:T(128)S(1)} %copy-done.8, bf16[384,1024]{1,0:T(8,128)(2,1)S(1)} %slice.53.query_ref, bf16[512,128]{1,0:T(8,128)(2,1)S(1)} %copy-done.7, bf16[512,128]{1,0:T(8,128)(2,1)S(1)} %copy-done.6, bf16[8,2,512,128]{3,2,1,0:T(8,128)(2,1)S(1)} %copy-done.1), custom_call_target="tpu_custom_call" | custom-call | flops 14495514624 | bytes 2359296 | tf_op jit(solution)/shard_map/attend_1_128/pallas_call | solution.py:177
  147.0 21.1 %convolution_convert_fusion = bf16[384,8192]{1,0:T(8,128)(2,1)} fusion(bf16[2048,8192]{1,0:T(8,128)(2,1)} %weight.1, bf16[384,1024]{1,0:T(8,128)(2,1)S(1)} %attend_1_128.1, bf16[128,1024]{1,0:T(8,128)(2,1)S(1)} %attend_0_384.1, bf16[256,1024]{1,0:T(8,128)(2,1)S(1)} %slice-done), kind=kOutput, calls=%fused_computation | convolution fusion | flops 12892766208 | bytes 41418752 | tf_op jit(solution)/shard_map/dot_general | solution.py:233
  168.1 0.0 reduce-scatter.5.cloned.1.call-update
  168.2 0.0 reduce-scatter.3.cloned.1.call-done
  168.2 112.6 %reduce-scatter.5.cloned.1.call-done = bf16[384,2048]{1,0:T(8,128)(2,1)} async-done(((bf16[384,8192]{1,0:T(8,128)(2,1)}), bf16[384,2048]{1,0:T(8,128)(2,1)}) %reduce-scatter.5.cloned.1.call-update) | async-done | bytes 1572880 | tf_op jit(solution)/shard_map/reduce_scatter | solution.py:234
  280.7 3.1 %pad_maximum_fusion = bf16[512,2048]{1,0:T(8,128)(2,1)} fusion(bf16[384,2048]{1,0:T(8,128)(2,1)} %reduce-scatter.5.cloned.1.call-done, bf16[128,2048]{1,0:T(8,128)(2,1)} %reduce-scatter.3.cloned.1.call-done), kind=kLoop, calls=%fused_computation.2 | loop fusion | flops 4194304 | bytes 4194304 | tf_op jit(solution)/shard_map/concatenate | solution.py:235
  (12 shorter events, 0.1 us)
Async XLA Ops:
  23.9 30.2 %all-to-all-start.1 = ((bf16[8,2,512,128]{3,2,1,0:T(8,128)(2,1)}), bf16[8,2,512,128]{3,2,1,0:T(8,128)(2,1)S(1)}, u32[]{:S(2)}, u32[]{:S(2)}) async-start(bf16[8,2,512,128]{3,2,1,0:T(8,128)(2,1)} %gather_0.1), calls=%async_computation.1 | async-start | bytes 4194304 | tf_op jit(solution)/shard_map/all_to_all | solution.py:206
  54.0 1.3 copy-start.2
  55.4 31.9 %all-to-all-start.2 = ((bf16[8,2,512,128]{3,2,1,0:T(8,128)(2,1)}), bf16[8,2,512,128]{3,2,1,0:T(8,128)(2,1)S(1)}, u32[]{:S(2)}, u32[]{:S(2)}) async-start(bf16[8,2,512,128]{3,2,1,0:T(8,128)(2,1)} %gather_1.1), calls=%async_computation.2 | async-start | bytes 4194304 | tf_op jit(solution)/shard_map/all_to_all | solution.py:206
  59.0 109.2 %reduce-scatter.3.cloned.1.call-start = ((), (), s32[]{:S(2)}) async-start(), calls=%async_computation.5 | async-start | bytes 2621440 | tf_op jit(solution)/shard_map/reduce_scatter | solution.py:231
  61.2 2.8 copy-start.9
  61.2 1.1 copy-start.10
  61.2 1.4 copy-start.11
  61.2 2.8 copy-start.3
  86.5 24.2 %copy-start.5 = (bf16[384,1024]{1,0:T(8,128)(2,1)}, bf16[384,1024]{1,0:T(8,128)(2,1)S(1)}, u32[]{:S(2)}) copy-start(bf16[384,1024]{1,0:T(8,128)(2,1)S(1)} %attend_0_0.1) | copy-start | bytes 2359300
  87.3 1.3 copy-start
  110.7 1.7 copy-start.4
  110.8 170.0 %reduce-scatter.5.cloned.1.call-start = ((), (), s32[]{:S(2)}) async-start(), calls=%async_computation.6 | async-start | bytes 7864320 | tf_op jit(solution)/shard_map/reduce_scatter | solution.py:234
  112.4 11.2 %copy-start.1 = (bf16[8,2,512,128]{3,2,1,0:T(8,128)(2,1)S(1)}, bf16[8,2,512,128]{3,2,1,0:T(8,128)(2,1)}, u32[]{:S(2)}) copy-start(bf16[8,2,512,128]{3,2,1,0:T(8,128)(2,1)} %copy-done) | copy-start | bytes 6291460
  112.4 11.3 %copy-start.6 = (bf16[512,128]{1,0:T(8,128)(2,1)S(1)}, bf16[512,128]{1,0:T(8,128)(2,1)}, u32[]{:S(2)}) copy-start(bf16[512,128]{1,0:T(8,128)(2,1)} %get-tuple-element.14.own_values) | copy-start | bytes 393220
  112.4 11.3 %copy-start.7 = (bf16[512,128]{1,0:T(8,128)(2,1)S(1)}, bf16[512,128]{1,0:T(8,128)(2,1)}, u32[]{:S(2)}) copy-start(bf16[512,128]{1,0:T(8,128)(2,1)} %get-tuple-element.21.own_keys) | copy-start | bytes 393220
  112.4 11.3 %copy-start.8 = (s32[8]{0:T(128)S(1)}, s32[8]{0:T(128)}, u32[]{:S(2)}) copy-start(s32[8]{0:T(128)} %get-tuple-element.18.owner_ref) | copy-start | bytes 100
  123.7 23.4 %slice-start = ((bf16[384,1024]{1,0:T(8,128)(2,1)}), bf16[256,1024]{1,0:T(8,128)(2,1)S(1)}, s32[]{:S(2)}) async-start(bf16[384,1024]{1,0:T(8,128)(2,1)} %copy-done.5), calls=%async_computation.7 | async-start | bytes 1048576 | tf_op jit(solution)/shard_map/slice | solution.py:224
Sparse Core Ops, SparseCore 0:
  110.9 45.2 reduce-scatter.2
  168.3 112.4 reduce-scatter.4
